TPU v7x, 32 devices: a whole 2x2x4 slice. The times are simulated.
32 devices in a mesh: row: 8 (over z, y), col: 4 (over x, core).
Axes of the slice: x: 2, y: 2, z: 4, core: 2. Of those that a mesh axis runs over, the one named last changes fastest.
Arguments:
- weights: bfloat16 [2, 8192, 8192], P(None, 'row', 'col'), may hold values from -0.0625 to 0.0625
- preact: float32 [2, 2, 8192], P(None, None, 'row'), may hold values from -2.5 to 2.5
- panel: bfloat16 [2, 64, 8192], P(None, None, 'col'), may hold values from -6 to 6
Outputs:
- basis_out: float32 [2, 64, 8192], P(None, None, 'col')
All inputs are finite; a program needn't handle non-finite values.
Results may differ from a plain program's by a relative error of at most 0.035.
Values may be sent and summed in bfloat16 or wider, within the bound.
A program may use at most 64 MiB of HBM per device.

v0:
```python
from functools import partial
import jax
import jax.numpy as jnp
from jax import lax
from jax.sharding import PartitionSpec as P

WIDTH = 8192
ITERS = 2


def on_device(weights, preact, panel):
    slopes = 1.0 - jnp.tanh(preact) ** 2
    layers = weights.shape[0]
    current = panel
    basis_out = panel.astype(jnp.float32)
    for iteration in range(ITERS):
        cotangent = None
        for layer_at in range(layers):
            partial_out = jnp.einsum(
                "bki,oi->bko", current, weights[layer_at], preferred_element_type=jnp.float32
            )
            summed = lax.psum_scatter(
                partial_out.astype(jnp.bfloat16), "col", scatter_dimension=1, tiled=True
            ).astype(jnp.float32)
            scaled = (slopes[:, layer_at, None, :] * summed).astype(jnp.bfloat16)
            if layer_at + 1 < layers:
                spread = lax.all_gather(scaled, "row", axis=2, tiled=True)
                current = lax.all_to_all(spread, "col", split_axis=2, concat_axis=1, tiled=True)
            else:
                cotangent = lax.all_gather(scaled, "col", axis=1, tiled=True)
        image_panel = None
        for layer_at in reversed(range(layers)):
            weighted = (slopes[:, layer_at, None, :] * cotangent).astype(jnp.bfloat16)
            partial_in = jnp.einsum(
                "bko,oi->bki", weighted, weights[layer_at], preferred_element_type=jnp.float32
            )
            if layer_at == 0:
                pieces = lax.psum_scatter(
                    partial_in.astype(jnp.bfloat16), "row", scatter_dimension=2, tiled=True
                )
                image_panel = lax.all_gather(pieces, "row", axis=2, tiled=True)
            else:
                pieces = lax.psum_scatter(
                    partial_in.astype(jnp.bfloat16), "row", scatter_dimension=1, tiled=True
                )
                spread = lax.all_gather(pieces, "col", axis=2, tiled=True)
                cotangent = lax.all_to_all(spread, "row", split_axis=2, concat_axis=1, tiled=True)
        local_gram = jnp.einsum(
            "bkw,bjw->bkj", image_panel, image_panel, preferred_element_type=jnp.float32
        )
        gram_sum = lax.psum(local_gram.astype(jnp.bfloat16), "col").astype(jnp.float32)
        factor = jnp.linalg.cholesky(gram_sum / WIDTH)
        basis_out = jax.vmap(partial(jax.scipy.linalg.solve_triangular, lower=True))(
            factor, image_panel.astype(jnp.float32)
        )
        current = basis_out.astype(jnp.bfloat16)
    return basis_out


def solution(mesh):
    return jax.shard_map(
        on_device,
        mesh=mesh,
        in_specs=(P(None, "row", "col"), P(None, None, "row"), P(None, None, "col")),
        out_specs=P(None, None, "col"),
        check_vma=False,
    )
```

profile of v0, /device:TPU:0, one launch (start us, length us, event | category | flops | bytes accessed | tf_op | source)
XLA Modules:
  0.0 776.8 jit_solution(17862595918340202358)
XLA Ops:
  6.5 1.0 copy-done
  7.6 4.4 fusion.40
  12.1 22.8 %reduce-scatter.13.cloned.1.call-done = bf16[2,16,1024]{2,1,0:T(8,128)(2,1)} async-done(((bf16[2,64,1024]{2,1,0:T(8,128)(2,1)}), bf16[2,16,1024]{2,1,0:T(8,128)(2,1)}) %reduce-scatter.13.cloned.1.call-update) | async-done | bytes 65552 | tf_op jit(solution)/shard_map/reduce_scatter | solution.py:22
  34.9 0.9 multiply_convert_fusion.7
  35.8 31.6 %all_gather.24 = bf16[2,16,8192]{2,1,0:T(8,128)(2,1)S(1)} all-gather(bf16[2,16,1024]{2,1,0:T(8,128)(2,1)S(1)} %multiply_convert_fusion.7), channel_id=1, replica_groups=mesh['row'=8,'col'=4] {'row'}, dimensions={2}, use_global_device_ids=true | all-gather | bytes 589824 | tf_op jit(solution)/shard_map/all_gather | solution.py:27
  67.4 6.7 copy.47
  74.1 5.8 reshape.23
  79.9 11.2 %all_to_all.54 = bf16[4,2,32768]{2,1,0:T(2,128)(2,1)S(1)} all-to-all(bf16[4,2,32768]{2,1,0:T(2,128)(2,1)S(1)} %reshape.23), channel_id=1, replica_groups=mesh['row'=8,'col'=4] {'col'}, dimensions={0} | all-to-all | bytes 1048576 | tf_op jit(solution)/shard_map/all_to_all | solution.py:28
  91.1 4.1 reshape.24
  95.2 9.7 %copy.67 = bf16[2,16,4,2048]{3,2,1,0:T(4,128)(2,1)S(1)} copy(bf16[2,16,4,2048]{1,0,3,2:T(2,128)(2,1)} %bitcast.105) | data formatting | bytes 1048576 | tf_op jit(solution)/shard_map/all_to_all | solution.py:28
  105.2 4.4 fusion.46
  109.7 20.0 %reduce-scatter.15.cloned.1.call-done = bf16[2,16,1024]{2,1,0:T(8,128)(2,1)} async-done(((bf16[2,64,1024]{2,1,0:T(8,128)(2,1)}), bf16[2,16,1024]{2,1,0:T(8,128)(2,1)}) %reduce-scatter.15.cloned.1.call-update) | async-done | bytes 65552 | tf_op jit(solution)/shard_map/reduce_scatter | solution.py:22
  129.8 0.9 multiply_convert_fusion.6
  130.6 5.8 all_gather.25
  136.4 2.9 fusion.34
  139.9 1.0 copy.75
  140.9 63.2 %reduce-scatter.25.cloned.1.call-done = bf16[8,4096]{1,0:T(8,128)(2,1)} async-done(((bf16[64,4096]{1,0:T(8,128)(2,1)}), bf16[8,4096]{1,0:T(8,128)(2,1)}) %reduce-scatter.25.cloned.1.call-update) | async-done | bytes 65552
  204.0 0.9 reshape.20
  204.9 5.8 all_gather.26
  210.7 6.7 copy.50
  217.4 6.4 reshape.25
  223.8 3.6 all-to-all-start.1
  227.8 9.0 %all-to-all-done.1 = bf16[8,2,8192]{2,1,0:T(2,128)(2,1)S(1)} async-done(((bf16[8,2,8192]{2,1,0:T(2,128)(2,1)}), bf16[8,2,8192]{2,1,0:T(2,128)(2,1)S(1)}, u32[]{:S(2)}, u32[]{:S(2)}) %all-to-all-start.1) | async-done | bytes 262176 | tf_op jit(solution)/shard_map/all_to_all | solution.py:47
  236.9 5.9 reshape.26
  242.8 7.5 fusion.2
  250.3 8.9 %copy.51 = bf16[2,8,8,1024]{3,2,1,0:T(8,128)(2,1)S(1)} copy(bf16[2,8,8,1024]{2,0,3,1:T(2,128)(2,1)} %fusion.2) | data formatting | bytes 524288 | tf_op jit(solution)/shard_map/convert_element_type | solution.py:33
  259.2 3.7 fusion.28
  263.0 62.1 %reduce-scatter.17.cloned.1.call-done = bf16[2,64,256]{2,1,0:T(8,128)(2,1)} async-done(((bf16[2,64,2048]{2,1,0:T(8,128)(2,1)}), bf16[2,64,256]{2,1,0:T(8,128)(2,1)}) %reduce-scatter.17.cloned.1.call-update) | async-done | bytes 65552 | tf_op jit(solution)/shard_map/reduce_scatter | solution.py:38
  325.1 31.8 %all_gather.27 = bf16[2,64,2048]{2,1,0:T(8,128)(2,1)S(1)} all-gather(bf16[2,64,256]{2,1,0:T(8,128)(2,1)} %reduce-scatter.17.cloned.1.call-done), channel_id=1, replica_groups=mesh['row'=8,'col'=4] {'row'}, dimensions={2}, use_global_device_ids=true | all-gather | bytes 589824 | tf_op jit(solution)/shard_map/all_gather | solution.py:41
  357.2 10.3 %psum.14 = bf16[2,64,64]{1,2,0:T(8,128)(2,1)S(1)} all-reduce(bf16[2,64,64]{1,2,0:T(8,128)(2,1)S(1)} %convolution_convert_fusion.2), channel_id=1, replica_groups=mesh['row'=8,'col'=4] {'col'}, use_global_device_ids=true, to_apply=%region_4.0 | all-reduce | flops 8192 | bytes 32768 | tf_op jit(solution)/shard_map/psum | solution.py:51
  367.6 11.7 %custom-call.8 = f32[2,64,64]{2,1,0:T(8,128)S(1)} custom-call(f32[2,64,64]{2,1,0:T(8,128)S(1)} %fusion.62), custom_call_target="Cholesky" | custom-call | tf_op jit(solution)/shard_map/jit(cholesky)/cholesky | solution.py:52
  379.6 9.8 %custom-call.9 = f32[2,1,64,64]{2,3,1,0:T(8,128)S(1)} custom-call(f32[2,1,64,64]{3,2,1,0:T(8,128)S(1)} %select_bitcast_fusion.1), custom_call_target="InvertDiagBlocksLowerTriangular" | custom-call | tf_op jit(solution)/shard_map/vmap(jit(_solve_triangular))/triangular_solve | solution.py:53
  389.4 1.1 convolution_convert_fusion
  390.5 4.4 fusion.43
  395.0 19.1 %reduce-scatter.19.cloned.1.call-done = bf16[2,16,1024]{2,1,0:T(8,128)(2,1)} async-done(((bf16[2,64,1024]{2,1,0:T(8,128)(2,1)}), bf16[2,16,1024]{2,1,0:T(8,128)(2,1)}) %reduce-scatter.19.cloned.1.call-update) | async-done | bytes 65552 | tf_op jit(solution)/shard_map/reduce_scatter | solution.py:22
  414.0 0.9 multiply_convert_fusion.5
  414.9 31.5 %all_gather.28 = bf16[2,16,8192]{2,1,0:T(8,128)(2,1)S(1)} all-gather(bf16[2,16,1024]{2,1,0:T(8,128)(2,1)S(1)} %multiply_convert_fusion.5), channel_id=1, replica_groups=mesh['row'=8,'col'=4] {'row'}, dimensions={2}, use_global_device_ids=true | all-gather | bytes 589824 | tf_op jit(solution)/shard_map/all_gather | solution.py:27
  446.4 6.7 copy.55
  453.1 5.8 reshape.27
  458.8 11.2 %all_to_all.55 = bf16[4,2,32768]{2,1,0:T(2,128)(2,1)S(1)} all-to-all(bf16[4,2,32768]{2,1,0:T(2,128)(2,1)S(1)} %reshape.27), channel_id=1, replica_groups=mesh['row'=8,'col'=4] {'col'}, dimensions={0} | all-to-all | bytes 1048576 | tf_op jit(solution)/shard_map/all_to_all | solution.py:28
  470.0 4.1 reshape.28
  474.2 9.7 %copy.68 = bf16[2,16,4,2048]{3,2,1,0:T(4,128)(2,1)S(1)} copy(bf16[2,16,4,2048]{1,0,3,2:T(2,128)(2,1)} %bitcast.107) | data formatting | bytes 1048576 | tf_op jit(solution)/shard_map/all_to_all | solution.py:28
  484.1 4.4 fusion.49
  488.7 20.2 %reduce-scatter.21.cloned.1.call-done = bf16[2,16,1024]{2,1,0:T(8,128)(2,1)} async-done(((bf16[2,64,1024]{2,1,0:T(8,128)(2,1)}), bf16[2,16,1024]{2,1,0:T(8,128)(2,1)}) %reduce-scatter.21.cloned.1.call-update) | async-done | bytes 65552 | tf_op jit(solution)/shard_map/reduce_scatter | solution.py:22
  508.9 0.9 multiply_convert_fusion.4
  509.7 5.8 all_gather.29
  515.5 2.9 fusion.37
  519.0 1.0 copy.76
  520.0 63.2 %reduce-scatter.27.cloned.1.call-done = bf16[8,4096]{1,0:T(8,128)(2,1)} async-done(((bf16[64,4096]{1,0:T(8,128)(2,1)}), bf16[8,4096]{1,0:T(8,128)(2,1)}) %reduce-scatter.27.cloned.1.call-update) | async-done | bytes 65552
  583.2 0.9 reshape.22
  584.1 5.8 all_gather.30
  589.9 6.7 copy.58
  596.6 5.8 reshape.29
  602.3 12.8 %all_to_all.56 = bf16[8,2,8192]{2,1,0:T(2,128)(2,1)S(1)} all-to-all(bf16[8,2,8192]{2,1,0:T(2,128)(2,1)S(1)} %reshape.29), channel_id=1, replica_groups=mesh['row'=8,'col'=4] {'row'}, dimensions={0} | all-to-all | bytes 524288 | tf_op jit(solution)/shard_map/all_to_all | solution.py:47
  615.2 5.9 reshape.30
  621.1 7.5 fusion.3
  628.6 8.9 %copy.59 = bf16[2,8,8,1024]{3,2,1,0:T(8,128)(2,1)S(1)} copy(bf16[2,8,8,1024]{2,0,3,1:T(2,128)(2,1)} %fusion.3) | data formatting | bytes 524288 | tf_op jit(solution)/shard_map/convert_element_type | solution.py:33
  637.5 3.8 fusion.31
  641.3 62.3 %reduce-scatter.23.cloned.1.call-done = bf16[2,64,256]{2,1,0:T(8,128)(2,1)} async-done(((bf16[2,64,2048]{2,1,0:T(8,128)(2,1)}), bf16[2,64,256]{2,1,0:T(8,128)(2,1)}) %reduce-scatter.23.cloned.1.call-update) | async-done | bytes 65552 | tf_op jit(solution)/shard_map/reduce_scatter | solution.py:38
  703.6 31.6 %all_gather.31 = bf16[2,64,2048]{2,1,0:T(8,128)(2,1)S(1)} all-gather(bf16[2,64,256]{2,1,0:T(8,128)(2,1)} %reduce-scatter.23.cloned.1.call-done), channel_id=1, replica_groups=mesh['row'=8,'col'=4] {'row'}, dimensions={2}, use_global_device_ids=true | all-gather | bytes 589824 | tf_op jit(solution)/shard_map/all_gather | solution.py:41
  735.5 10.5 %psum.15 = bf16[2,64,64]{1,2,0:T(8,128)(2,1)S(1)} all-reduce(bf16[2,64,64]{1,2,0:T(8,128)(2,1)S(1)} %convolution_convert_fusion.1), channel_id=1, replica_groups=mesh['row'=8,'col'=4] {'col'}, use_global_device_ids=true, to_apply=%region_11.14 | all-reduce | flops 8192 | bytes 32768 | tf_op jit(solution)/shard_map/psum | solution.py:51
  746.2 11.7 %custom-call.10 = f32[2,64,64]{2,1,0:T(8,128)S(1)} custom-call(f32[2,64,64]{2,1,0:T(8,128)S(1)} %fusion.60), custom_call_target="Cholesky" | custom-call | tf_op jit(solution)/shard_map/jit(cholesky)/cholesky | solution.py:52
  758.1 9.8 %custom-call.11 = f32[2,1,64,64]{2,3,1,0:T(8,128)S(1)} custom-call(f32[2,1,64,64]{3,2,1,0:T(8,128)S(1)} %select_bitcast_fusion), custom_call_target="InvertDiagBlocksLowerTriangular" | custom-call | tf_op jit(solution)/shard_map/vmap(jit(_solve_triangular))/triangular_solve | solution.py:53
  768.0 2.0 fusion.52
  (48 shorter events, 3.8 us)
Async XLA Ops:
  6.5 1.0 copy-start
  6.5 5.5 copy-start.2
  6.5 28.4 %reduce-scatter.13.cloned.1.call-start = ((), (), s32[]{:S(2)}) async-start(), calls=%async_computation.12 | async-start | bytes 327680 | tf_op jit(solution)/shard_map/reduce_scatter | solution.py:22
  12.0 117.8 %reduce-scatter.15.cloned.1.call-start = ((), (), s32[]{:S(2)}) async-start(), calls=%async_computation.13 | async-start | bytes 327680 | tf_op jit(solution)/shard_map/reduce_scatter | solution.py:22
  109.7 94.4 %reduce-scatter.25.cloned.1.call-start = ((), (), s32[]{:S(2)}) async-start(), calls=%async_computation.18 | async-start | bytes 589824
  223.8 13.1 %all-to-all-start.1 = ((bf16[8,2,8192]{2,1,0:T(2,128)(2,1)}), bf16[8,2,8192]{2,1,0:T(2,128)(2,1)S(1)}, u32[]{:S(2)}, u32[]{:S(2)}) async-start(bf16[8,2,8192]{2,1,0:T(2,128)(2,1)} %reshape.25), calls=%async_computation.3 | async-start | bytes 524288 | tf_op jit(solution)/shard_map/all_to_all | solution.py:47
  227.4 97.7 %reduce-scatter.17.cloned.1.call-start = ((), (), s32[]{:S(2)}) async-start(), calls=%async_computation.14 | async-start | bytes 589824 | tf_op jit(solution)/shard_map/reduce_scatter | solution.py:38
  262.9 151.1 %reduce-scatter.19.cloned.1.call-start = ((), (), s32[]{:S(2)}) async-start(), calls=%async_computation.15 | async-start | bytes 327680 | tf_op jit(solution)/shard_map/reduce_scatter | solution.py:22
  394.9 113.9 %reduce-scatter.21.cloned.1.call-start = ((), (), s32[]{:S(2)}) async-start(), calls=%async_computation.16 | async-start | bytes 327680 | tf_op jit(solution)/shard_map/reduce_scatter | solution.py:22
  488.6 94.6 %reduce-scatter.27.cloned.1.call-start = ((), (), s32[]{:S(2)}) async-start(), calls=%async_computation.19 | async-start | bytes 589824
  519.9 183.6 %reduce-scatter.23.cloned.1.call-start = ((), (), s32[]{:S(2)}) async-start(), calls=%async_computation.17 | async-start | bytes 589824 | tf_op jit(solution)/shard_map/reduce_scatter | solution.py:38
  637.5 132.5 %copy-start.1 = (bf16[2,64,2048]{2,1,0:T(8,128)(2,1)S(1)}, bf16[2,64,2048]{2,1,0:T(8,128)(2,1)}, u32[]{:S(2)}) copy-start(bf16[2,64,2048]{2,1,0:T(8,128)(2,1)} %param.8) | copy-start | bytes 1572868
Sparse Core Ops, SparseCore 0:
  12.1 22.7 reduce-scatter.12
  109.8 19.9 reduce-scatter.14
  141.0 63.0 reduce-scatter.24
  263.1 62.0 reduce-scatter.16
  395.0 18.9 reduce-scatter.18
  488.7 20.0 reduce-scatter.20
  520.1 63.1 reduce-scatter.26
  641.4 62.1 reduce-scatter.22
where the time goes:
time: 779 us; the launch traced here: 777 us
  waiting for transfers between devices  342 us (44%)
  blocking collectives  206 us (26%)
  local copies, waits for them, and re-layouts  114 us (15%)
  other arithmetic  62.1 us (8%)
  matrix products  34.7 us (4%)
  between operations  13.8 us (2%)
    unnamed x10, waiting for transfers between devices  127 us
    reduce_scatter x2, waiting for transfers between devices, on_device(): lax.psum_scatter(partial_in.astype(jnp.bfloat16), 'row', scatter_dimensio...  124 us
    reduce_scatter x4, waiting for transfers between devices, on_device(): lax.psum_scatter(partial_out.astype(jnp.bfloat16), 'col', scatter_dimensi...  82.1 us
    all_gather x2, blocking collectives, on_device(): image_panel = lax.all_gather(pieces, 'row', axis=2, tiled=True)  63.4 us
    all_gather x2, blocking collectives, on_device(): spread = lax.all_gather(scaled, 'row', axis=2, tiled=True)  63.1 us
    unnamed x24, local copies, waits for them, and re-layouts  49.6 us
    another operation x7, other arithmetic, on_device(): factor = jnp.linalg.cholesky(gram_sum / WIDTH)  23.8 us
    all_to_all x2, blocking collectives, on_device(): lax.all_to_all(spread, 'col', split_axis=2, concat_axis=1, tiled=True)  22.4 us
  transfers between devices with their start and end apart: 9, of which 9 were waited for; matrix products, arithmetic and copies ran while one was open for 0% of the time, Pallas kernels for 0%

commit v1 on v0

--- a/solution.py
+++ b/solution.py
@@ -24,7 +24,15 @@
             ).astype(jnp.float32)
             scaled = (slopes[:, layer_at, None, :] * summed).astype(jnp.bfloat16)
             if layer_at + 1 < layers:
-                spread = lax.all_gather(scaled, "row", axis=2, tiled=True)
+                spread = jnp.concatenate(
+                    lax.all_to_all(
+                        jnp.stack([scaled for _ in range(lax.axis_size("row"))], axis=0),
+                        "row",
+                        0,
+                        0,
+                    ),
+                    axis=2,
+                )
                 current = lax.all_to_all(spread, "col", split_axis=2, concat_axis=1, tiled=True)
             else:
                 cotangent = lax.all_gather(scaled, "col", axis=1, tiled=True)

time: 779 us -> 753 us (0.967)
  blocking collectives: 206 us -> 182 us
    all_gather x2 -> x0, blocking collectives: 63.1 us -> none  [on_device(): spread = lax.all_gather(scaled, 'row', axis=2, tiled=True)]
    all_to_all x0 -> x2, blocking collectives: none -> 39.2 us  [on_device(): lax.all_to_all(jnp.stack([scaled for _ in range(lax.axis_size('row'))], a...]
    reshape x0 -> x2, local copies, waits for them, and re-layouts: none -> 14.5 us  [on_device(): jnp.concatenate(lax.all_to_all(jnp.stack([scaled for _ in range(lax.axis_...]
    all_gather x2 -> x0, local copies, waits for them, and re-layouts: 13.4 us -> none  [on_device(): spread = lax.all_gather(scaled, 'row', axis=2, tiled=True)]
where the time goes in v1:
time: 753 us; the launch traced here: 750 us
  waiting for transfers between devices  339 us (45%)
  blocking collectives  182 us (24%)
  local copies, waits for them, and re-layouts  116 us (15%)
  other arithmetic  62.1 us (8%)
  matrix products  34.7 us (5%)
  between operations  13.8 us (2%)
    unnamed x10, waiting for transfers between devices  127 us
    reduce_scatter x2, waiting for transfers between devices, on_device(): lax.psum_scatter(partial_in.astype(jnp.bfloat16), 'row', scatter_dimensio...  124 us
    reduce_scatter x4, waiting for transfers between devices, on_device(): lax.psum_scatter(partial_out.astype(jnp.bfloat16), 'col', scatter_dimensi...  78.6 us
    all_gather x2, blocking collectives, on_device(): image_panel = lax.all_gather(pieces, 'row', axis=2, tiled=True)  63.3 us
    unnamed x24, local copies, waits for them, and re-layouts  49.6 us
    all_to_all x2, blocking collectives, on_device(): lax.all_to_all(jnp.stack([scaled for _ in range(lax.axis_size('row'))], a...  39.2 us
    another operation x7, other arithmetic, on_device(): factor = jnp.linalg.cholesky(gram_sum / WIDTH)  23.8 us
    all_to_all x2, blocking collectives, on_device(): lax.all_to_all(spread, 'col', split_axis=2, concat_axis=1, tiled=True)  22.4 us
  transfers between devices with their start and end apart: 9, of which 9 were waited for; matrix products, arithmetic and copies ran while one was open for 0% of the time, Pallas kernels for 0%

profile of v1, /device:TPU:0, one launch (start us, length us, event | category | flops | bytes accessed | tf_op | source)
XLA Modules:
  0.0 750.4 jit_solution(4201843655188856507)
XLA Ops:
  6.5 1.0 copy-done
  7.6 4.4 fusion.40
  12.1 22.8 %reduce-scatter.13.cloned.1.call-done = bf16[2,16,1024]{2,1,0:T(8,128)(2,1)} async-done(((bf16[2,64,1024]{2,1,0:T(8,128)(2,1)}), bf16[2,16,1024]{2,1,0:T(8,128)(2,1)}) %reduce-scatter.13.cloned.1.call-update) | async-done | bytes 65552 | tf_op jit(solution)/shard_map/reduce_scatter | solution.py:22
  34.9 0.9 multiply_convert_fusion.7
  35.9 19.6 %all_to_all.64 = bf16[8,2,16,1024]{3,2,1,0:T(8,128)(2,1)S(1)} all-to-all(bf16[8,2,16,1024]{3,2,1,0:T(8,128)(2,1)S(1)} %stack.4), channel_id=1, replica_groups=mesh['row'=8,'col'=4] {'row'}, dimensions={0} | all-to-all | bytes 1048576 | tf_op jit(solution)/shard_map/all_to_all | solution.py:28
  55.4 7.2 copy.73
  62.7 5.8 reshape.43
  68.4 11.2 %all_to_all.65 = bf16[4,2,32768]{2,1,0:T(2,128)(2,1)S(1)} all-to-all(bf16[4,2,32768]{2,1,0:T(2,128)(2,1)S(1)} %reshape.43), channel_id=1, replica_groups=mesh['row'=8,'col'=4] {'col'}, dimensions={0} | all-to-all | bytes 1048576 | tf_op jit(solution)/shard_map/all_to_all | solution.py:36
  79.6 4.1 reshape.44
  83.8 9.7 %copy.74 = bf16[2,16,4,2048]{3,2,1,0:T(4,128)(2,1)S(1)} copy(bf16[2,16,4,2048]{1,0,3,2:T(2,128)(2,1)} %bitcast.109) | data formatting | bytes 1048576 | tf_op jit(solution)/shard_map/all_to_all | solution.py:36
  93.7 4.4 fusion.46
  98.3 18.3 %reduce-scatter.15.cloned.1.call-done = bf16[2,16,1024]{2,1,0:T(8,128)(2,1)} async-done(((bf16[2,64,1024]{2,1,0:T(8,128)(2,1)}), bf16[2,16,1024]{2,1,0:T(8,128)(2,1)}) %reduce-scatter.15.cloned.1.call-update) | async-done | bytes 65552 | tf_op jit(solution)/shard_map/reduce_scatter | solution.py:22
  116.6 0.9 multiply_convert_fusion.6
  117.4 5.8 all_gather.18
  123.2 2.9 fusion.34
  126.7 1.0 copy.85
  127.6 63.2 %reduce-scatter.25.cloned.1.call-done = bf16[8,4096]{1,0:T(8,128)(2,1)} async-done(((bf16[64,4096]{1,0:T(8,128)(2,1)}), bf16[8,4096]{1,0:T(8,128)(2,1)}) %reduce-scatter.25.cloned.1.call-update) | async-done | bytes 65552
  190.9 0.9 reshape.40
  191.8 5.8 all_gather.19
  197.6 6.7 copy.55
  204.2 6.4 reshape.45
  210.6 3.6 all-to-all-start.2
  214.7 9.0 %all-to-all-done.2 = bf16[8,2,8192]{2,1,0:T(2,128)(2,1)S(1)} async-done(((bf16[8,2,8192]{2,1,0:T(2,128)(2,1)}), bf16[8,2,8192]{2,1,0:T(2,128)(2,1)S(1)}, u32[]{:S(2)}, u32[]{:S(2)}) %all-to-all-start.2) | async-done | bytes 262176 | tf_op jit(solution)/shard_map/all_to_all | solution.py:55
  223.7 5.9 reshape.46
  229.6 7.5 %fusion.2 = bf16[2,8,8,1024]{2,0,3,1:T(2,128)(2,1)} fusion(bf16[2,8,8,1024]{1,0,3,2:T(2,128)(2,1)} %bitcast.114, f32[2,1024]{0,1:T(8,128)S(1)} %copy.50), kind=kLoop, calls=%fused_computation.4 | loop fusion | flops 393216 | bytes 532480 | tf_op jit(solution)/shard_map/convert_element_type | solution.py:41
  237.2 8.9 %copy.56 = bf16[2,8,8,1024]{3,2,1,0:T(8,128)(2,1)S(1)} copy(bf16[2,8,8,1024]{2,0,3,1:T(2,128)(2,1)} %fusion.2) | data formatting | bytes 524288 | tf_op jit(solution)/shard_map/convert_element_type | solution.py:41
  246.0 3.7 fusion.28
  249.9 62.1 %reduce-scatter.17.cloned.1.call-done = bf16[2,64,256]{2,1,0:T(8,128)(2,1)} async-done(((bf16[2,64,2048]{2,1,0:T(8,128)(2,1)}), bf16[2,64,256]{2,1,0:T(8,128)(2,1)}) %reduce-scatter.17.cloned.1.call-update) | async-done | bytes 65552 | tf_op jit(solution)/shard_map/reduce_scatter | solution.py:46
  312.0 31.7 %all_gather.20 = bf16[2,64,2048]{2,1,0:T(8,128)(2,1)S(1)} all-gather(bf16[2,64,256]{2,1,0:T(8,128)(2,1)} %reduce-scatter.17.cloned.1.call-done), channel_id=1, replica_groups=mesh['row'=8,'col'=4] {'row'}, dimensions={2}, use_global_device_ids=true | all-gather | bytes 589824 | tf_op jit(solution)/shard_map/all_gather | solution.py:49
  343.9 10.3 %psum.14 = bf16[2,64,64]{1,2,0:T(8,128)(2,1)S(1)} all-reduce(bf16[2,64,64]{1,2,0:T(8,128)(2,1)S(1)} %convolution_convert_fusion.2), channel_id=1, replica_groups=mesh['row'=8,'col'=4] {'col'}, use_global_device_ids=true, to_apply=%region_4.0 | all-reduce | flops 8192 | bytes 32768 | tf_op jit(solution)/shard_map/psum | solution.py:59
  354.3 11.7 %custom-call.8 = f32[2,64,64]{2,1,0:T(8,128)S(1)} custom-call(f32[2,64,64]{2,1,0:T(8,128)S(1)} %fusion.62), custom_call_target="Cholesky" | custom-call | tf_op jit(solution)/shard_map/jit(cholesky)/cholesky | solution.py:60
  366.3 9.8 %custom-call.9 = f32[2,1,64,64]{2,3,1,0:T(8,128)S(1)} custom-call(f32[2,1,64,64]{3,2,1,0:T(8,128)S(1)} %select_bitcast_fusion.1), custom_call_target="InvertDiagBlocksLowerTriangular" | custom-call | tf_op jit(solution)/shard_map/vmap(jit(_solve_triangular))/triangular_solve | solution.py:61
  376.1 1.1 convolution_convert_fusion
  377.2 4.4 fusion.43
  381.7 19.2 %reduce-scatter.19.cloned.1.call-done = bf16[2,16,1024]{2,1,0:T(8,128)(2,1)} async-done(((bf16[2,64,1024]{2,1,0:T(8,128)(2,1)}), bf16[2,16,1024]{2,1,0:T(8,128)(2,1)}) %reduce-scatter.19.cloned.1.call-update) | async-done | bytes 65552 | tf_op jit(solution)/shard_map/reduce_scatter | solution.py:22
  400.9 0.9 multiply_convert_fusion.5
  401.9 19.6 %all_to_all.66 = bf16[8,2,16,1024]{3,2,1,0:T(8,128)(2,1)S(1)} all-to-all(bf16[8,2,16,1024]{3,2,1,0:T(8,128)(2,1)S(1)} %stack.5), channel_id=1, replica_groups=mesh['row'=8,'col'=4] {'row'}, dimensions={0} | all-to-all | bytes 1048576 | tf_op jit(solution)/shard_map/all_to_all | solution.py:28
  421.4 7.2 copy.75
  428.7 5.8 reshape.47
  434.4 11.2 %all_to_all.67 = bf16[4,2,32768]{2,1,0:T(2,128)(2,1)S(1)} all-to-all(bf16[4,2,32768]{2,1,0:T(2,128)(2,1)S(1)} %reshape.47), channel_id=1, replica_groups=mesh['row'=8,'col'=4] {'col'}, dimensions={0} | all-to-all | bytes 1048576 | tf_op jit(solution)/shard_map/all_to_all | solution.py:36
  445.7 4.1 reshape.48
  449.8 9.7 %copy.76 = bf16[2,16,4,2048]{3,2,1,0:T(4,128)(2,1)S(1)} copy(bf16[2,16,4,2048]{1,0,3,2:T(2,128)(2,1)} %bitcast.111) | data formatting | bytes 1048576 | tf_op jit(solution)/shard_map/all_to_all | solution.py:36
  459.8 4.4 fusion.49
  464.3 18.3 %reduce-scatter.21.cloned.1.call-done = bf16[2,16,1024]{2,1,0:T(8,128)(2,1)} async-done(((bf16[2,64,1024]{2,1,0:T(8,128)(2,1)}), bf16[2,16,1024]{2,1,0:T(8,128)(2,1)}) %reduce-scatter.21.cloned.1.call-update) | async-done | bytes 65552 | tf_op jit(solution)/shard_map/reduce_scatter | solution.py:22
  482.5 0.9 multiply_convert_fusion.4
  483.4 5.8 all_gather.21
  489.2 2.9 fusion.37
  492.6 1.0 copy.86
  493.7 63.2 %reduce-scatter.27.cloned.1.call-done = bf16[8,4096]{1,0:T(8,128)(2,1)} async-done(((bf16[64,4096]{1,0:T(8,128)(2,1)}), bf16[8,4096]{1,0:T(8,128)(2,1)}) %reduce-scatter.27.cloned.1.call-update) | async-done | bytes 65552
  556.9 0.9 reshape.42
  557.8 5.8 all_gather.22
  563.5 6.7 copy.64
  570.2 5.8 reshape.49
  576.0 12.8 %all_to_all.68 = bf16[8,2,8192]{2,1,0:T(2,128)(2,1)S(1)} all-to-all(bf16[8,2,8192]{2,1,0:T(2,128)(2,1)S(1)} %reshape.49), channel_id=1, replica_groups=mesh['row'=8,'col'=4] {'row'}, dimensions={0} | all-to-all | bytes 524288 | tf_op jit(solution)/shard_map/all_to_all | solution.py:55
  588.8 5.9 reshape.50
  594.7 7.5 %fusion.3 = bf16[2,8,8,1024]{2,0,3,1:T(2,128)(2,1)} fusion(bf16[2,8,8,1024]{1,0,3,2:T(2,128)(2,1)} %bitcast.112, f32[2,1024]{0,1:T(8,128)S(1)} %copy.50), kind=kLoop, calls=%fused_computation.5 | loop fusion | flops 393216 | bytes 532480 | tf_op jit(solution)/shard_map/convert_element_type | solution.py:41
  602.2 8.9 %copy.65 = bf16[2,8,8,1024]{3,2,1,0:T(8,128)(2,1)S(1)} copy(bf16[2,8,8,1024]{2,0,3,1:T(2,128)(2,1)} %fusion.3) | data formatting | bytes 524288 | tf_op jit(solution)/shard_map/convert_element_type | solution.py:41
  611.1 3.8 fusion.31
  614.9 62.2 %reduce-scatter.23.cloned.1.call-done = bf16[2,64,256]{2,1,0:T(8,128)(2,1)} async-done(((bf16[2,64,2048]{2,1,0:T(8,128)(2,1)}), bf16[2,64,256]{2,1,0:T(8,128)(2,1)}) %reduce-scatter.23.cloned.1.call-update) | async-done | bytes 65552 | tf_op jit(solution)/shard_map/reduce_scatter | solution.py:46
  677.1 31.6 %all_gather.23 = bf16[2,64,2048]{2,1,0:T(8,128)(2,1)S(1)} all-gather(bf16[2,64,256]{2,1,0:T(8,128)(2,1)} %reduce-scatter.23.cloned.1.call-done), channel_id=1, replica_groups=mesh['row'=8,'col'=4] {'row'}, dimensions={2}, use_global_device_ids=true | all-gather | bytes 589824 | tf_op jit(solution)/shard_map/all_gather | solution.py:49
  709.1 10.5 %psum.15 = bf16[2,64,64]{1,2,0:T(8,128)(2,1)S(1)} all-reduce(bf16[2,64,64]{1,2,0:T(8,128)(2,1)S(1)} %convolution_convert_fusion.1), channel_id=1, replica_groups=mesh['row'=8,'col'=4] {'col'}, use_global_device_ids=true, to_apply=%region_11.14 | all-reduce | flops 8192 | bytes 32768 | tf_op jit(solution)/shard_map/psum | solution.py:59
  719.7 11.7 %custom-call.10 = f32[2,64,64]{2,1,0:T(8,128)S(1)} custom-call(f32[2,64,64]{2,1,0:T(8,128)S(1)} %fusion.60), custom_call_target="Cholesky" | custom-call | tf_op jit(solution)/shard_map/jit(cholesky)/cholesky | solution.py:60
  731.7 9.8 %custom-call.11 = f32[2,1,64,64]{2,3,1,0:T(8,128)S(1)} custom-call(f32[2,1,64,64]{3,2,1,0:T(8,128)S(1)} %select_bitcast_fusion), custom_call_target="InvertDiagBlocksLowerTriangular" | custom-call | tf_op jit(solution)/shard_map/vmap(jit(_solve_triangular))/triangular_solve | solution.py:61
  741.5 2.0 fusion.52
  (50 shorter events, 3.9 us)
Async XLA Ops:
  6.5 1.0 copy-start
  6.5 5.5 copy-start.2
  6.5 28.4 %reduce-scatter.13.cloned.1.call-start = ((), (), s32[]{:S(2)}) async-start(), calls=%async_computation.14 | async-start | bytes 327680 | tf_op jit(solution)/shard_map/reduce_scatter | solution.py:22
  12.0 104.5 %reduce-scatter.15.cloned.1.call-start = ((), (), s32[]{:S(2)}) async-start(), calls=%async_computation.15 | async-start | bytes 327680 | tf_op jit(solution)/shard_map/reduce_scatter | solution.py:22
  98.2 92.7 %reduce-scatter.25.cloned.1.call-start = ((), (), s32[]{:S(2)}) async-start(), calls=%async_computation.20 | async-start | bytes 589824
  210.6 13.1 %all-to-all-start.2 = ((bf16[8,2,8192]{2,1,0:T(2,128)(2,1)}), bf16[8,2,8192]{2,1,0:T(2,128)(2,1)S(1)}, u32[]{:S(2)}, u32[]{:S(2)}) async-start(bf16[8,2,8192]{2,1,0:T(2,128)(2,1)} %reshape.45), calls=%async_computation.4 | async-start | bytes 524288 | tf_op jit(solution)/shard_map/all_to_all | solution.py:55
  214.2 97.7 %reduce-scatter.17.cloned.1.call-start = ((), (), s32[]{:S(2)}) async-start(), calls=%async_computation.16 | async-start | bytes 589824 | tf_op jit(solution)/shard_map/reduce_scatter | solution.py:46
  249.8 151.2 %reduce-scatter.19.cloned.1.call-start = ((), (), s32[]{:S(2)}) async-start(), calls=%async_computation.17 | async-start | bytes 327680 | tf_op jit(solution)/shard_map/reduce_scatter | solution.py:22
  381.6 100.9 %reduce-scatter.21.cloned.1.call-start = ((), (), s32[]{:S(2)}) async-start(), calls=%async_computation.18 | async-start | bytes 327680 | tf_op jit(solution)/shard_map/reduce_scatter | solution.py:22
  464.2 92.6 %reduce-scatter.27.cloned.1.call-start = ((), (), s32[]{:S(2)}) async-start(), calls=%async_computation.21 | async-start | bytes 589824
  493.6 183.5 %reduce-scatter.23.cloned.1.call-start = ((), (), s32[]{:S(2)}) async-start(), calls=%async_computation.19 | async-start | bytes 589824 | tf_op jit(solution)/shard_map/reduce_scatter | solution.py:46
  611.1 132.4 %copy-start.1 = (bf16[2,64,2048]{2,1,0:T(8,128)(2,1)S(1)}, bf16[2,64,2048]{2,1,0:T(8,128)(2,1)}, u32[]{:S(2)}) copy-start(bf16[2,64,2048]{2,1,0:T(8,128)(2,1)} %param.8) | copy-start | bytes 1572868
Sparse Core Ops, SparseCore 0:
  12.1 22.7 reduce-scatter.12
  98.3 18.1 reduce-scatter.14
  127.8 63.0 reduce-scatter.24
  249.9 62.0 reduce-scatter.16
  381.8 19.1 reduce-scatter.18
  464.3 18.1 reduce-scatter.20
  493.7 63.0 reduce-scatter.26
  615.0 62.0 reduce-scatter.22
